TPU v7x, 128 devices: a whole 4x4x4 slice. The times are simulated.
128 devices in a mesh: ctx: 8 (over z, core), tp: 16 (over x, y).
Axes of the slice: x: 4, y: 4, z: 4, core: 2. Of those that a mesh axis runs over, the one named last changes fastest.
Arguments:
- inputs: bfloat16 [2048, 8192], P(('ctx', 'tp')), may hold values from -6 to 6
- query_weight: bfloat16 [8192, 8192], P(None, 'tp'), may hold values from -0.0625 to 0.0625
- key_weight: bfloat16 [8192, 8192], P(None, 'tp'), may hold values from -0.0625 to 0.0625
- value_weight: bfloat16 [8192, 8192], P(None, 'tp'), may hold values from -0.0625 to 0.0625
- filter_taps: float32 [128, 8192], P(None, 'tp'), may hold values from -0.45 to 0.45
- out_grad: bfloat16 [2048, 8192], P('ctx', 'tp'), may hold values from -1.5 to 1.5
Outputs:
- mixed: bfloat16 [2048, 8192], P('ctx', 'tp')
- inputs_grad: bfloat16 [2048, 8192], P(('ctx', 'tp'))
- filter_grad: float32 [128, 8192], P(None, 'tp')
All inputs are finite; a program needn't handle non-finite values.
Results may differ from a plain program's by a relative error of at most 0.025.
Values may be sent and summed in bfloat16 or wider, within the bound.
A program may use at most 128 MiB of HBM per device.

v0:
```python
import jax
import jax.numpy as jnp
from jax import lax
from jax.sharding import PartitionSpec as P


def from_behind(block, axis, distance):
    devices = range(lax.axis_size(axis))
    route = [(i - distance, i) for i in devices if i - distance in devices]
    return lax.ppermute(block, axis, route)


def forward_filter(padded, filter_taps, length):
    taps = filter_taps.shape[0]
    total = jnp.zeros((length, padded.shape[1]), jnp.float32)
    for offset in range(taps):
        start = taps - 1 - offset
        total = total + filter_taps[offset] * padded[start : start + length]
    return total


def backward_filter(padded, filter_taps, length):
    taps = filter_taps.shape[0]
    total = jnp.zeros((length, padded.shape[1]), jnp.float32)
    for offset in range(taps):
        total = total + filter_taps[offset] * padded[offset : offset + length]
    return total


def tap_products(grad_rows, padded, taps, length):
    rows_out = []
    for offset in range(taps):
        start = taps - 1 - offset
        rows_out.append(jnp.sum(grad_rows * padded[start : start + length], axis=0))
    return jnp.stack(rows_out)


def contract(left, right):
    return lax.dot_general(
        left, right, (((1,), (1,)), ((), ())), preferred_element_type=jnp.float32
    )


def on_device(inputs, query_weight, key_weight, value_weight, filter_taps, out_grad):
    group = query_weight.shape[1]
    taps = filter_taps.shape[0]
    margin = taps - 1
    own_rows = inputs.shape[0]
    piece = lax.all_gather(inputs, "tp", axis=0, tiled=True)
    query_part = jnp.dot(piece, query_weight, preferred_element_type=jnp.float32)
    keys_part = jnp.dot(piece, key_weight, preferred_element_type=jnp.float32)
    values_part = jnp.dot(piece, value_weight, preferred_element_type=jnp.float32)
    projected = jnp.concatenate([query_part, keys_part, values_part], axis=1).astype(jnp.bfloat16)
    length = projected.shape[0]
    query = projected[:, :group]
    keys = projected[:, group : 2 * group]
    values = projected[:, 2 * group :]
    product = (keys.astype(jnp.float32) * values.astype(jnp.float32)).astype(jnp.bfloat16)
    grad_f32 = out_grad.astype(jnp.float32)
    conv_in_grad = (grad_f32 * query.astype(jnp.float32)).astype(jnp.bfloat16)
    tail_part = from_behind(product[length - margin :], "ctx", 1)
    head_part = from_behind(conv_in_grad[:margin], "ctx", -1)
    padded_prod = jnp.concatenate([tail_part, product], axis=0).astype(jnp.float32)
    conv = forward_filter(padded_prod, filter_taps, length)
    mixed = (query.astype(jnp.float32) * conv).astype(jnp.bfloat16)
    query_grad = (grad_f32 * conv).astype(jnp.bfloat16)
    padded_grad = jnp.concatenate([conv_in_grad, head_part], axis=0).astype(jnp.float32)
    product_grad = backward_filter(padded_grad, filter_taps, length)
    keys_grad = (product_grad * values.astype(jnp.float32)).astype(jnp.bfloat16)
    values_grad = (product_grad * keys.astype(jnp.float32)).astype(jnp.bfloat16)
    local_taps = tap_products(conv_in_grad.astype(jnp.float32), padded_prod, taps, length)
    filter_grad = lax.psum(local_taps.astype(jnp.bfloat16), "ctx").astype(jnp.float32)
    query_rows = lax.slice_in_dim(query_grad, 0, lax.axis_size("tp") * own_rows, axis=0)
    keys_rows = lax.slice_in_dim(keys_grad, 0, lax.axis_size("tp") * own_rows, axis=0)
    values_rows = lax.slice_in_dim(values_grad, 0, lax.axis_size("tp") * own_rows, axis=0)
    total = contract(query_rows, query_weight)
    total = total + contract(keys_rows, key_weight)
    summed = lax.psum_scatter(
        (total + contract(values_rows, value_weight)).astype(jnp.bfloat16),
        "tp",
        scatter_dimension=0,
        tiled=True,
    )
    return (mixed, summed, filter_grad)


def solution(mesh):
    in_specs = (
        P(("ctx", "tp"), None),
        P(None, "tp"),
        P(None, "tp"),
        P(None, "tp"),
        P(None, "tp"),
        P("ctx", "tp"),
    )
    out_specs = (P("ctx", "tp"), P(("ctx", "tp"), None), P(None, "tp"))
    return jax.shard_map(
        on_device, mesh=mesh, in_specs=in_specs, out_specs=out_specs, check_vma=False
    )
```

profile of v0, /device:TPU:1, one launch (start us, length us, event | category | flops | bytes accessed | tf_op | source)
XLA Modules:
  0.0 266.8 jit_solution(11515920868183889877)
XLA Ops:
  7.2 0.0 all-gather.2.cloned.1.call-start
  7.2 0.7 all-gather.2.cloned.1.call-update
  7.9 0.0 all-reduce.2.cloned.1.call-start
  7.9 1.2 fusion.268
  9.2 1.3 fusion.267
  10.4 1.2 fusion.266
  11.7 1.2 fusion.265
  12.9 1.1 fusion.264
  14.0 1.7 fusion.269
  15.7 49.0 %all-gather.2.cloned.1.call-done = bf16[256,8192]{1,0:T(8,128)(2,1)} async-done(((bf16[16,8192]{1,0:T(8,128)(2,1)}), bf16[256,8192]{1,0:T(8,128)(2,1)}) %all-gather.2.cloned.1.call-update) | async-done | bytes 4194320 | tf_op jit(solution)/shard_map/all_gather | solution.py:49
  64.8 7.1 %fusion.1 = f32[256,512]{1,0:T(8,128)S(1)} fusion(bf16[256,8192]{1,0:T(8,128)(2,1)} %all-gather.2.cloned.1.call-done, bf16[8192,512]{1,0:T(8,128)(2,1)} %param.9), kind=kOutput, calls=%fused_computation.132 | convolution fusion | flops 2147745792 | bytes 13107200 | tf_op jit(solution)/shard_map/dot_general | solution.py:52
  71.9 0.0 copy-done.20
  71.9 0.0 copy-start.2
  71.9 0.0 slice-start.1
  71.9 6.8 %multiply_convert_fusion.3 = (bf16[256,512]{1,0:T(8,128)(2,1)S(1)}, f32[256,512]{1,0:T(8,128)}) fusion(f32[256,512]{1,0:T(8,128)S(1)} %fusion.1, bf16[256,8192]{1,0:T(8,128)(2,1)S(1)} %copy-done.20, bf16[8192,512]{1,0:T(8,128)(2,1)} %param.8), kind=kOutput, calls=%fused_computation.528 | convolution fusion | flops 2148007936 | bytes 13893632 | tf_op jit(solution)/shard_map/dot_general | solution.py:51
  78.7 0.0 copy-done.2
  78.8 3.7 %collective-permute-start = (bf16[127,512]{1,0:T(8,128)(2,1)S(1)}, bf16[127,512]{1,0:T(8,128)(2,1)S(1)}, u32[]{:S(2)}, u32[]{:S(2)}) collective-permute-start(bf16[127,512]{1,0:T(8,128)(2,1)S(1)} %slice.1812), channel_id=1, source_target_pairs={{0,16},{16,32},{32,48},{48,64},{64,80},{80,96},{96,112},{1,17},{17... | collective-permute-start | bytes 390152 | tf_op jit(solution)/shard_map/ppermute | solution.py:10
  82.5 1.7 fusion.270
  84.2 0.2 collective-permute-done
  84.4 0.1 maximum_convert_fusion
  84.5 0.0 slice-done
  84.5 0.0 slice-done.1
  84.6 0.0 copy-start
  84.6 16.5 %multiply_convert_fusion.2 = (bf16[256,512]{1,0:T(8,128)(2,1)}, f32[256,512]{1,0:T(8,128)}, f32[256,512]{1,0:T(8,128)}) fusion(f32[383,512]{1,0:T(8,128)S(1)} %maximum_convert_fusion, f32[512]{0:T(512)} %bitcast.391, f32[512]{0:T(512)} %bitcast.393, f32[512]{0:T(512)S(1)} %bitcast.293, f32[512]{0:T(512)S(1)} %bitcast.295, f32[512]{0:T(512)S(1)} %bitcast.297, ...), kind=kOutput, calls=%fused_computation.526 | convolution fusion | flops 2181431296 | bytes 81264640 | tf_op jit(solution)/shard_map/dot_general | solution.py:50
  101.1 0.0 copy-done
  101.1 2.1 fusion.127
  103.2 0.2 fusion.126
  103.4 1.0 fusion.128
  104.4 1.0 fusion.129
  105.4 1.0 fusion.130
  106.5 1.1 fusion.131
  107.5 0.0 copy-start.4
  107.5 1.1 fusion.132
  108.6 1.0 fusion.133
  111.1 10.1 %stack.644 = bf16[128,512]{1,0:T(8,128)(2,1)} concatenate(bf16[1,512]{1,0:T(2,128)(2,1)S(1)} %stack.516, bf16[1,512]{1,0:T(2,128)(2,1)S(1)} %stack.517, bf16[1,512]{1,0:T(2,128)(2,1)S(1)} %stack.518, bf16[1,512]{1,0:T(2,128)(2,1)S(1)} %stack.519, bf16[1,512]{1,0:T(2,128)(2,1)S(1)} %stack.520, bf16[1,512]{1,0:T(2,128)(2,1)S(1)} %stack.521, bf16[1,512]{1,0:T(2,128)(2,1)S(1)} %stack.522, ...), dimensions={0} | concatenate | bytes 262144 | tf_op jit(solution)/shard_map/stack | solution.py:35
  121.2 0.0 all-reduce.2.cloned.1.call-update
  121.3 0.0 reduce-scatter.2.cloned.1.call-start
  121.3 1.9 collective-permute-start.1
  123.3 0.0 copy-done.4
  123.3 0.0 copy-start.5
  123.3 0.0 copy-start.6
  123.3 0.0 copy-start.7
  123.3 0.0 copy-start.8
  123.3 0.0 copy-start.9
  123.3 0.0 copy-start.10
  123.3 0.0 copy-start.11
  123.3 0.0 copy-start.12
  123.3 0.0 copy-start.13
  123.4 0.0 copy-start.14
  123.4 0.0 copy-start.15
  123.4 0.0 copy-start.16
  123.4 0.0 copy-start.17
  123.4 0.0 copy-start.18
  123.4 0.0 copy-start.19
  123.4 5.8 %fusion.261 = f32[256,8192]{1,0:T(8,128)S(1)} fusion(bf16[8192,512]{1,0:T(8,128)(2,1)} %param.7, f32[256,512]{1,0:T(8,128)S(1)} %copy-done.4, bf16[256,512]{1,0:T(8,128)(2,1)S(1)} %copy-done), kind=kOutput, calls=%fused_computation.532 | convolution fusion | flops 2147876864 | bytes 17563648 | tf_op jit(solution)/shard_map/dot_general | solution.py:39
  129.2 0.0 collective-permute-done.1
  129.2 0.1 maximum_convert_fusion.1
  129.4 12.3 %fusion.134 = f32[256,512]{1,0:T(8,128)S(1)} fusion(f32[383,512]{1,0:T(8,128)S(1)} %maximum_convert_fusion.1, f32[512]{0:T(512)S(1)} %bitcast.392, f32[512]{0:T(512)S(1)} %bitcast.394, f32[512]{0:T(512)S(1)} %bitcast.294, f32[512]{0:T(512)S(1)} %bitcast.296, f32[512]{0:T(512)S(1)} %bitcast.298, f32[512]{0:T(512)S(1)} %bitcast.300, f32[512]{0:T(512)S(1)} %bitcast.302, ...), kind=kLoop, calls=%fused_computation.270 | loop fusion | flops 33423360 | bytes 67895296 | tf_op jit(solution)/shard_map/add | solution.py:26
  141.8 9.1 %convolution_add_fusion.1 = f32[256,8192]{1,0:T(8,128)} fusion(f32[256,8192]{1,0:T(8,128)S(1)} %fusion.261, bf16[8192,512]{1,0:T(8,128)(2,1)} %param.8, f32[256,512]{1,0:T(8,128)S(1)} %fusion.134, f32[256,512]{1,0:T(8,128)S(1)} %copy-done.3), kind=kOutput, calls=%fused_computation.129 | convolution fusion | flops 2149842944 | bytes 26214400 | tf_op jit(solution)/shard_map/dot_general | solution.py:39
  150.9 10.1 %fusion = bf16[256,8192]{1,0:T(8,128)(2,1)} fusion(f32[256,8192]{1,0:T(8,128)} %convolution_add_fusion.1, bf16[8192,512]{1,0:T(8,128)(2,1)} %param.9, f32[256,512]{1,0:T(8,128)S(1)} %fusion.134, f32[256,512]{1,0:T(8,128)S(1)} %copy-done.1), kind=kOutput, calls=%fused_computation.130 | convolution fusion | flops 2151940096 | bytes 22020096 | tf_op jit(solution)/shard_map/dot_general | solution.py:39
  161.0 0.0 reduce-scatter.2.cloned.1.call-update
  161.1 18.0 %all-reduce.2.cloned.1.call-done = bf16[128,512]{1,0:T(8,128)(2,1)} async-done(((bf16[128,512]{1,0:T(8,128)(2,1)}), bf16[128,512]{1,0:T(8,128)(2,1)}) %all-reduce.2.cloned.1.call-update) | async-done | bytes 131088 | tf_op jit(solution)/shard_map/psum | solution.py:72
  179.1 1.6 convert_element_type.64
  180.7 79.5 %reduce-scatter.2.cloned.1.call-done = bf16[16,8192]{1,0:T(8,128)(2,1)} async-done(((bf16[256,8192]{1,0:T(8,128)(2,1)}), bf16[16,8192]{1,0:T(8,128)(2,1)}) %reduce-scatter.2.cloned.1.call-update) | async-done | bytes 262160 | tf_op jit(solution)/shard_map/reduce_scatter | solution.py:78
  (152 shorter events, 0.7 us)
Async XLA Ops:
  7.2 57.6 %all-gather.2.cloned.1.call-start = ((), (), s32[]{:S(2)}) async-start(), calls=%async_computation.1 | async-start | bytes 4456448 | tf_op jit(solution)/shard_map/all_gather | solution.py:49
  7.9 171.2 %all-reduce.2.cloned.1.call-start = ((), (), s32[]{:S(2)}) async-start(), calls=%async_computation.3 | async-start | bytes 262144 | tf_op jit(solution)/shard_map/psum | solution.py:72
  64.8 7.1 %copy-start.20 = (bf16[256,8192]{1,0:T(8,128)(2,1)S(1)}, bf16[256,8192]{1,0:T(8,128)(2,1)}, u32[]{:S(2)}) copy-start(bf16[256,8192]{1,0:T(8,128)(2,1)} %all-gather.2.cloned.1.call-done) | copy-start | bytes 12582916
  64.8 19.7 %slice-start = ((s8[8388608]{0:T(1024)(128)(4,1)}), s8[4194304]{0:T(1024)(128)(4,1)S(1)}, s32[]{:S(2)}) async-start(s8[8388608]{0:T(1024)(128)(4,1)} %bitcast.137), calls=%async_computation.4 | async-start | bytes 8388608
  71.9 6.8 %copy-start.2 = (f32[256,512]{1,0:T(8,128)}, f32[256,512]{1,0:T(8,128)S(1)}, u32[]{:S(2)}) copy-start(f32[256,512]{1,0:T(8,128)S(1)} %fusion.1) | copy-start | bytes 1572868
  71.9 12.6 %slice-start.1 = ((s8[8388608]{0:T(1024)(128)(4,1)}), s8[4194304]{0:T(1024)(128)(4,1)S(1)}, s32[]{:S(2)}) async-start(s8[8388608]{0:T(1024)(128)(4,1)} %bitcast.137), calls=%async_computation.5 | async-start | bytes 8388608
  78.8 5.7 %collective-permute-start = (bf16[127,512]{1,0:T(8,128)(2,1)S(1)}, bf16[127,512]{1,0:T(8,128)(2,1)S(1)}, u32[]{:S(2)}, u32[]{:S(2)}) collective-permute-start(bf16[127,512]{1,0:T(8,128)(2,1)S(1)} %slice.1812), channel_id=1, source_target_pairs={{0,16},{16,32},{32,48},{48,64},{64,80},{80,96},{96,112},{1,17},{17... | collective-permute-start | bytes 390152 | tf_op jit(solution)/shard_map/ppermute | solution.py:10
  84.6 16.6 %copy-start = (bf16[256,512]{1,0:T(8,128)(2,1)S(1)}, bf16[256,512]{1,0:T(8,128)(2,1)}, u32[]{:S(2)}) copy-start(bf16[256,512]{1,0:T(8,128)(2,1)} %param.11) | copy-start | bytes 786436
  107.5 15.7 %copy-start.4 = (f32[256,512]{1,0:T(8,128)S(1)}, f32[256,512]{1,0:T(8,128)}, u32[]{:S(2)}) copy-start(f32[256,512]{1,0:T(8,128)} %get-tuple-element.133) | copy-start | bytes 1572868
  121.3 139.0 %reduce-scatter.2.cloned.1.call-start = ((), (), s32[]{:S(2)}) async-start(), calls=%async_computation.2 | async-start | bytes 4456448 | tf_op jit(solution)/shard_map/reduce_scatter | solution.py:78
  121.3 7.9 %collective-permute-start.1 = (bf16[127,512]{1,0:T(8,128)(2,1)S(1)}, bf16[127,512]{1,0:T(8,128)(2,1)S(1)}, u32[]{:S(2)}, u32[]{:S(2)}) collective-permute-start(bf16[127,512]{1,0:T(8,128)(2,1)S(1)} %slice.1941), channel_id=1, source_target_pairs={{16,0},{32,16},{48,32},{64,48},{80,64},{96,80},{112,96},{17,1},{33... | collective-permute-start | bytes 390152 | tf_op jit(solution)/shard_map/ppermute | solution.py:10
  123.3 6.0 %copy-start.5 = (f32[1,512]{1,0:T(1,128)S(1)}, f32[1,512]{1,0:T(1,128)}, u32[]{:S(2)}) copy-start(f32[1,512]{1,0:T(1,128)} %get-tuple-element.247) | copy-start | bytes 6148
  123.3 6.0 %copy-start.6 = (f32[1,512]{1,0:T(1,128)S(1)}, f32[1,512]{1,0:T(1,128)}, u32[]{:S(2)}) copy-start(f32[1,512]{1,0:T(1,128)} %get-tuple-element.248) | copy-start | bytes 6148
  123.3 6.0 %copy-start.7 = (f32[1,512]{1,0:T(1,128)S(1)}, f32[1,512]{1,0:T(1,128)}, u32[]{:S(2)}) copy-start(f32[1,512]{1,0:T(1,128)} %get-tuple-element.249) | copy-start | bytes 6148
  123.3 6.0 %copy-start.8 = (f32[1,512]{1,0:T(1,128)S(1)}, f32[1,512]{1,0:T(1,128)}, u32[]{:S(2)}) copy-start(f32[1,512]{1,0:T(1,128)} %get-tuple-element.250) | copy-start | bytes 6148
  123.3 6.0 %copy-start.9 = (f32[1,512]{1,0:T(1,128)S(1)}, f32[1,512]{1,0:T(1,128)}, u32[]{:S(2)}) copy-start(f32[1,512]{1,0:T(1,128)} %get-tuple-element.251) | copy-start | bytes 6148
  123.3 6.0 %copy-start.10 = (f32[1,512]{1,0:T(1,128)S(1)}, f32[1,512]{1,0:T(1,128)}, u32[]{:S(2)}) copy-start(f32[1,512]{1,0:T(1,128)} %get-tuple-element.252) | copy-start | bytes 6148
  123.3 6.0 %copy-start.11 = (f32[1,512]{1,0:T(1,128)S(1)}, f32[1,512]{1,0:T(1,128)}, u32[]{:S(2)}) copy-start(f32[1,512]{1,0:T(1,128)} %get-tuple-element.253) | copy-start | bytes 6148
  123.3 6.0 %copy-start.12 = (f32[1,512]{1,0:T(1,128)S(1)}, f32[1,512]{1,0:T(1,128)}, u32[]{:S(2)}) copy-start(f32[1,512]{1,0:T(1,128)} %get-tuple-element.254) | copy-start | bytes 6148
  123.3 6.0 %copy-start.13 = (f32[1,512]{1,0:T(1,128)S(1)}, f32[1,512]{1,0:T(1,128)}, u32[]{:S(2)}) copy-start(f32[1,512]{1,0:T(1,128)} %get-tuple-element.255) | copy-start | bytes 6148
  123.4 6.0 %copy-start.14 = (f32[1,512]{1,0:T(1,128)S(1)}, f32[1,512]{1,0:T(1,128)}, u32[]{:S(2)}) copy-start(f32[1,512]{1,0:T(1,128)} %get-tuple-element.256) | copy-start | bytes 6148
  123.4 6.0 %copy-start.15 = (f32[1,512]{1,0:T(1,128)S(1)}, f32[1,512]{1,0:T(1,128)}, u32[]{:S(2)}) copy-start(f32[1,512]{1,0:T(1,128)} %get-tuple-element.257) | copy-start | bytes 6148
  123.4 6.0 %copy-start.16 = (f32[1,512]{1,0:T(1,128)S(1)}, f32[1,512]{1,0:T(1,128)}, u32[]{:S(2)}) copy-start(f32[1,512]{1,0:T(1,128)} %get-tuple-element.258) | copy-start | bytes 6148
  123.4 6.0 %copy-start.17 = (f32[1,512]{1,0:T(1,128)S(1)}, f32[1,512]{1,0:T(1,128)}, u32[]{:S(2)}) copy-start(f32[1,512]{1,0:T(1,128)} %get-tuple-element.259) | copy-start | bytes 6148
  123.4 6.0 %copy-start.18 = (f32[1,512]{1,0:T(1,128)S(1)}, f32[1,512]{1,0:T(1,128)}, u32[]{:S(2)}) copy-start(f32[1,512]{1,0:T(1,128)} %get-tuple-element.260) | copy-start | bytes 6148
  123.4 6.0 %copy-start.19 = (f32[1,512]{1,0:T(1,128)S(1)}, f32[1,512]{1,0:T(1,128)}, u32[]{:S(2)}) copy-start(f32[1,512]{1,0:T(1,128)} %get-tuple-element.261) | copy-start | bytes 6148
  129.4 12.4 %copy-start.3 = (f32[256,512]{1,0:T(8,128)S(1)}, f32[256,512]{1,0:T(8,128)}, u32[]{:S(2)}) copy-start(f32[256,512]{1,0:T(8,128)} %copy-done.2) | copy-start | bytes 1572868
  141.8 9.1 %copy-start.1 = (f32[256,512]{1,0:T(8,128)S(1)}, f32[256,512]{1,0:T(8,128)}, u32[]{:S(2)}) copy-start(f32[256,512]{1,0:T(8,128)} %get-tuple-element.263) | copy-start | bytes 1572868
Sparse Core Ops, SparseCore 0:
  10.1 54.5 all-gather.1
  121.4 57.6 all-reduce.1
  183.4 76.8 reduce-scatter.1
where the time goes:
time: 269 us; the launch traced here: 267 us
  waiting for transfers between devices  148 us (55%)
  matrix products  55.4 us (21%)
  other arithmetic  22.6 us (8%)
  local copies, waits for them, and re-layouts  20.4 us (8%)
  between operations  15.1 us (6%)
  starting transfers between devices  5.78 us (2%)
    reduce_scatter x1, waiting for transfers between devices, on_device(): lax.psum_scatter((total + contract(values_rows, value_weight)).astype(jnp...  79.5 us
    all_gather x1, waiting for transfers between devices, on_device(): piece = lax.all_gather(inputs, 'tp', axis=0, tiled=True)  49 us
    dot_general x3, matrix products, contract(): lax.dot_general(left, right, (((1,), (1,)), ((), ())), preferred_element_...  25 us
    psum x1, waiting for transfers between devices, on_device(): lax.psum(local_taps.astype(jnp.bfloat16), 'ctx').astype(jnp.float32)  18 us
    dot_general x1, matrix products, on_device(): jnp.dot(piece, query_weight, preferred_element_type=jnp.float32)  16.5 us
    add x1, other arithmetic, backward_filter(): total = total + filter_taps[offset] * padded[offset:offset + length]  12.3 us
    another operation x129, local copies, waits for them, and re-layouts, tap_products(): return jnp.stack(rows_out)  10.8 us
    slice x7, local copies, waits for them, and re-layouts, forward_filter(): total = total + filter_taps[offset] * padded[start:start + length]  9.45 us
  transfers between devices with their start and end apart: 5, of which 4 were waited for; matrix products, arithmetic and copies ran while one was open for 18% of the time, Pallas kernels for 0%

commit v1 on v0

v1 whole, which is shorter than its diff:
```python
import jax
import jax.numpy as jnp
import numpy as np
from jax import lax
from jax.experimental import pallas as pl
from jax.experimental.pallas import tpu as pltpu
from jax.sharding import PartitionSpec as P

MESH = pl.DeviceIdType.MESH
BF, F32 = jnp.bfloat16, jnp.float32
SIDE = 4
ROWS = 16
D = 8192
GROUP = 512
BLOCK = 256
TAPS = 128
N_CTX = 8
FREQ = 192
POINTS = 2 * FREQ
GATHER = (2048, 2048, 1536, 1536, 512, 512)
SCATTER = (512, 512, 1024, 1024, 1024, 1024, 1024, 1024, 512, 512)


def starts(widths):
    return [sum(widths[:i]) for i in range(len(widths))]


def transforms():
    angle = np.pi / POINTS * np.outer(2 * np.arange(FREQ) + 1, np.arange(POINTS))
    forward = np.concatenate([np.cos(angle), -np.sin(angle)], axis=0)
    back = forward.T * (2.0 / POINTS)
    lags = TAPS - np.arange(TAPS)
    inverse = np.concatenate([back[TAPS:], back[:BLOCK], back[lags]], axis=0)
    return jnp.asarray(forward, BF), jnp.asarray(inverse, BF)


def dot(a, b):
    return jnp.dot(a, b, preferred_element_type=F32)


def kernel(
    inp, wq, wk, wv, taps_in, og_in, fwd_in, inv_in,
    mixed_out, grad_out, filt_out,
    X, W, acc, og, taps, fm, im, qkv, prod, cig, hx, hc, xs, hs, co, cs, conv, G,
    mixed, PB, R1H, R1, R2H, R2, gout, fpart, FR, FO,
    own_sem, w_sem, in_sem, out_sem, ag_send, ag_recv, halo_send, halo_recv, rs_send, rs_recv,
    f_send, f_recv,
):
    ctx = lax.axis_index("ctx")
    tp = lax.axis_index("tp")
    x = tp // SIDE
    y = tp % SIDE

    def coord(dim, shift=0):
        return ((x if dim == 0 else y) + shift) % SIDE

    def near(dim, d):
        s = 1 if d == 0 else SIDE - 1
        if dim == 0:
            return {"tp": coord(0, s) * SIDE + y}
        return {"tp": x * SIDE + coord(1, s)}

    own_copies = [pltpu.make_async_copy(inp, X.at[x, y], own_sem)]
    loads = []
    for s, c0 in enumerate(starts(GATHER)):
        cols = pl.ds(c0, GATHER[s])
        loads.append([
            pltpu.make_async_copy(w.at[cols, :], W.at[i, cols, :], w_sem.at[s, i])
            for i, w in enumerate((wq, wk, wv))
        ])
    small = [
        pltpu.make_async_copy(src, dst, in_sem.at[i])
        for i, (src, dst) in enumerate(((fwd_in, fm), (taps_in, taps), (inv_in, im), (og_in, og)))
    ]
    own_copies[0].start()
    for group in loads:
        for c in group:
            c.start()
    for c in small:
        c.start()

    barrier = pltpu.get_barrier_semaphore()
    for dim in range(2):
        for d in range(2):
            pl.semaphore_signal(barrier, inc=1, device_id=near(dim, d), device_id_type=MESH)
    for k in range(1, N_CTX):
        pl.semaphore_signal(barrier, inc=1, device_id={"ctx": (ctx + k) % N_CTX}, device_id_type=MESH)
    pl.semaphore_wait(barrier, 4 + N_CTX - 1)
    own_copies[0].wait()

    def gather_copy(s, kind, d):
        t = s % 2
        c0, kw = starts(GATHER)[s], GATHER[s]
        whole, half = pl.ds(c0, kw), pl.ds(c0 + d * (kw // 2), kw // 2)
        back = SIDE - 1 if d == 0 else 1
        if kind == 0:
            ref, dim = X.at[x, y, :, whole], t
        elif kind == 1:
            c = coord(t, back)
            ref, dim = (X.at[c, y, :, half] if t == 0 else X.at[x, c, :, half]), t
        elif kind == 2:
            ref, dim = (X.at[:, y, :, whole] if t == 0 else X.at[x, :, :, whole]), 1 - t
        else:
            c = coord(1 - t, back)
            ref, dim = (X.at[:, c, :, half] if t == 0 else X.at[c, :, :, half]), 1 - t
        return pltpu.make_async_remote_copy(
            src_ref=ref, dst_ref=ref, send_sem=ag_send.at[s, kind, d], recv_sem=ag_recv.at[s, kind, d],
            device_id=near(dim, d), device_id_type=MESH,
        )

    def gather_stage(s, kind):
        for d in range(2):
            if kind in (1, 3):
                gather_copy(s, kind - 1, d).wait_recv()
            gather_copy(s, kind, d).start()

    def gather_wait(s, kind):
        for d in range(2):
            gather_copy(s, kind, d).wait_recv()

    def project(s):
        c0, kw = starts(GATHER)[s], GATHER[s]
        for c in loads[s]:
            c.wait()

        def one(i, carry):
            w = (i + 1) % 3
            part = dot(X[:, :, :, c0 : c0 + kw].reshape(BLOCK, kw), W[w, c0 : c0 + kw, :])
            if s == 0:
                acc[w] = part
            else:
                acc[w] += part
            return carry

        lax.fori_loop(0, 3, one, 0)

    n = len(GATHER)
    for s in range(n):
        gather_stage(s, 0)
    for c in small:
        c.wait()
    tap = taps[...]
    tap_hi = tap.astype(BF)
    tap_lo = (tap - tap_hi.astype(F32)).astype(BF)
    hs[...] = dot(fm[:, :TAPS], tap_hi) + dot(fm[:, :TAPS], tap_lo)
    for s in range(n):
        gather_stage(s, 1)
        if s >= 2:
            gather_wait(s - 2, 1)
            gather_stage(s - 2, 2)
    for s in (n - 2, n - 1):
        gather_wait(s, 1)
        gather_stage(s, 2)
    gather_stage(0, 3)
    gather_stage(1, 3)
    for s in range(n):
        if s + 2 < n:
            gather_stage(s + 2, 3)
        gather_wait(s, 3)
        project(s)

    qkv[1] = acc[1].astype(BF)
    qkv[2] = acc[2].astype(BF)
    prod[...] = (qkv[1].astype(F32) * qkv[2].astype(F32)).astype(BF)
    tail = pltpu.make_async_remote_copy(
        src_ref=prod.at[pl.ds(BLOCK - TAPS, TAPS)], dst_ref=hx, send_sem=halo_send.at[0], recv_sem=halo_recv.at[0],
        device_id={"ctx": (ctx + 1) % N_CTX}, device_id_type=MESH,
    )
    tail.start()
    qkv[0] = acc[0].astype(BF)
    cig[...] = (og[...].astype(F32) * qkv[0].astype(F32)).astype(BF)
    head = pltpu.make_async_remote_copy(
        src_ref=cig.at[pl.ds(0, TAPS)], dst_ref=hc, send_sem=halo_send.at[1], recv_sem=halo_recv.at[1],
        device_id={"ctx": (ctx + N_CTX - 1) % N_CTX}, device_id_type=MESH,
    )
    head.start()
    xs[...] = dot(fm[:, TAPS:], prod[...])
    co[...] = dot(fm[:, :BLOCK], cig[...])
    for s in range(n):
        for kind in range(4):
            for d in range(2):
                gather_copy(s, kind, d).wait_send()

    h_re, h_im = hs.at[pl.ds(0, FREQ)], hs.at[pl.ds(FREQ, FREQ)]
    tail.wait_recv()
    halo = hx[...]
    xs[...] += dot(fm[:, :TAPS], jnp.where(ctx > 0, halo, jnp.zeros_like(halo)))
    x_re, x_im = xs.at[pl.ds(0, FREQ)], xs.at[pl.ds(FREQ, FREQ)]
    spec = jnp.concatenate(
        [x_re[...] * h_re[...] - x_im[...] * h_im[...], x_re[...] * h_im[...] + x_im[...] * h_re[...]], axis=0
    ).astype(BF)
    conv[...] = dot(im[:BLOCK, :], spec)
    G[0] = (og[...].astype(F32) * conv[...]).astype(BF)
    head.wait_recv()
    halo = hc[...]
    cs[...] = co[...] + dot(fm[:, BLOCK:], jnp.where(ctx < N_CTX - 1, halo, jnp.zeros_like(halo)))
    c_re, c_im = cs.at[pl.ds(0, FREQ)], cs.at[pl.ds(FREQ, FREQ)]
    spec = jnp.concatenate(
        [c_re[...] * h_re[...] + c_im[...] * h_im[...], c_im[...] * h_re[...] - c_re[...] * h_im[...]], axis=0
    ).astype(BF)
    back = dot(im[BLOCK : 2 * BLOCK, :], spec)
    G[1] = (back * qkv[2].astype(F32)).astype(BF)
    G[2] = (back * qkv[1].astype(F32)).astype(BF)

    def scatter_copy(s, kind, d):
        t = s % 2
        c0, kw = starts(SCATTER)[s], SCATTER[s]
        whole, half = pl.ds(c0, kw), pl.ds(c0 + d * (kw // 2), kw // 2)
        ahead = 1 if d == 0 else SIDE - 1
        if kind == 0:
            c, dim = coord(1 - t, 2), 1 - t
            src, dst = (PB.at[:, c, :, half] if t == 0 else PB.at[c, :, :, half]), R1H.at[:, :, half]
        elif kind == 1:
            c, dim = coord(1 - t, ahead), 1 - t
            src, dst = (PB.at[:, c, :, whole] if t == 0 else PB.at[c, :, :, whole]), R1.at[d, :, :, whole]
        elif kind == 2:
            c, dim = coord(t, 2), t
            src, dst = (PB.at[c, y, :, half] if t == 0 else PB.at[x, c, :, half]), R2H.at[:, half]
        else:
            c, dim = coord(t, ahead), t
            src, dst = (PB.at[c, y, :, whole] if t == 0 else PB.at[x, c, :, whole]), R2.at[d, :, whole]
        return pltpu.make_async_remote_copy(
            src_ref=src, dst_ref=dst, send_sem=rs_send.at[s, kind, d], recv_sem=rs_recv.at[s, kind, d],
            device_id=near(dim, d), device_id_type=MESH,
        )

    def produce(s):
        c0, kw = starts(SCATTER)[s], SCATTER[s]
        total = None
        for w in range(3):
            part = lax.dot_general(
                G[w], W[w, c0 : c0 + kw, :], (((1,), (1,)), ((), ())), preferred_element_type=F32
            )
            total = part if total is None else total + part
        PB[:, :, :, c0 : c0 + kw] = total.astype(BF).reshape(SIDE, SIDE, ROWS, kw)
        for d in range(2):
            scatter_copy(s, 0, d).start()

    def add_half_block(s):
        t = s % 2
        c0, kw = starts(SCATTER)[s], SCATTER[s]
        for d in range(2):
            half = slice(c0 + d * (kw // 2), c0 + (d + 1) * (kw // 2))
            c = coord(1 - t, 1 if d == 0 else SIDE - 1)
            scatter_copy(s, 0, d).wait_recv()
            got = R1H[:, :, half].astype(F32)
            if t == 0:
                PB[:, c, :, half] = (PB[:, c, :, half].astype(F32) + got).astype(BF)
            else:
                PB[c, :, :, half] = (PB[c, :, :, half].astype(F32) + got).astype(BF)
            scatter_copy(s, 1, d).start()

    def add_blocks(s):
        t = s % 2
        c0, kw = starts(SCATTER)[s], SCATTER[s]
        cols = slice(c0, c0 + kw)
        for d in range(2):
            scatter_copy(s, 1, d).wait_recv()
        got = R1[0, :, :, cols].astype(F32) + R1[1, :, :, cols].astype(F32)
        if t == 0:
            PB[:, y, :, cols] = (PB[:, y, :, cols].astype(F32) + got).astype(BF)
        else:
            PB[x, :, :, cols] = (PB[x, :, :, cols].astype(F32) + got).astype(BF)
        for d in range(2):
            scatter_copy(s, 2, d).start()

    def add_half_rows(s):
        t = s % 2
        c0, kw = starts(SCATTER)[s], SCATTER[s]
        for d in range(2):
            half = slice(c0 + d * (kw // 2), c0 + (d + 1) * (kw // 2))
            c = coord(t, 1 if d == 0 else SIDE - 1)
            scatter_copy(s, 2, d).wait_recv()
            got = R2H[:, half].astype(F32)
            if t == 0:
                PB[c, y, :, half] = (PB[c, y, :, half].astype(F32) + got).astype(BF)
            else:
                PB[x, c, :, half] = (PB[x, c, :, half].astype(F32) + got).astype(BF)
            scatter_copy(s, 3, d).start()

    def finish(s):
        c0, kw = starts(SCATTER)[s], SCATTER[s]
        cols = slice(c0, c0 + kw)
        for d in range(2):
            scatter_copy(s, 3, d).wait_recv()
        gout[:, cols] = (
            PB[x, y, :, cols].astype(F32) + R2[0, :, cols].astype(F32) + R2[1, :, cols].astype(F32)
        ).astype(BF)

    def piece_copy(k):
        to = (ctx + k) % N_CTX
        return pltpu.make_async_remote_copy(
            src_ref=fpart.at[to], dst_ref=FR.at[k], send_sem=f_send.at[0, k], recv_sem=f_recv.at[0, k],
            device_id={"ctx": to}, device_id_type=MESH,
        )

    def share_copy(k):
        return pltpu.make_async_remote_copy(
            src_ref=FO.at[ctx], dst_ref=FO.at[ctx], send_sem=f_send.at[1, k], recv_sem=f_recv.at[1, k],
            device_id={"ctx": (ctx + k) % N_CTX}, device_id_type=MESH,
        )

    def share_arrival(k):
        slot = (ctx + N_CTX - k) % N_CTX
        return pltpu.make_async_remote_copy(
            src_ref=FO.at[slot], dst_ref=FO.at[slot], send_sem=f_send.at[1, k], recv_sem=f_recv.at[1, k],
            device_id={"ctx": (ctx + k) % N_CTX}, device_id_type=MESH,
        )

    def filter_start():
        o_re, o_im = co.at[pl.ds(0, FREQ)], co.at[pl.ds(FREQ, FREQ)]
        spec = jnp.concatenate(
            [x_re[...] * o_re[...] + x_im[...] * o_im[...], x_im[...] * o_re[...] - x_re[...] * o_im[...]], axis=0
        ).astype(BF)
        fpart[...] = dot(im[2 * BLOCK :, :], spec).reshape(N_CTX, TAPS // N_CTX, GROUP)
        for k in range(1, N_CTX):
            piece_copy(k).start()

    def filter_sum():
        total = fpart[ctx]
        for k in range(1, N_CTX):
            piece_copy(k).wait_recv()
            total = total + FR[k]
        FO[ctx] = total
        for k in range(1, N_CTX):
            share_copy(k).start()

    mixed_copy = pltpu.make_async_copy(mixed, mixed_out, out_sem.at[0])
    m = len(SCATTER)
    lag = 2
    for s in range(m + 4 * lag):
        if s < m:
            produce(s)
        for stage, fn in enumerate((add_half_block, add_blocks, add_half_rows, finish)):
            j = s - (stage + 1) * lag
            if 0 <= j < m:
                fn(j)
        if s == 3:
            filter_start()
        if s == 5:
            mixed[...] = (qkv[0].astype(F32) * conv[...]).astype(BF)
            mixed_copy.start()
        if s == 8:
            filter_sum()
    grad_copy = pltpu.make_async_copy(gout, grad_out, out_sem.at[1])
    grad_copy.start()
    for k in range(1, N_CTX):
        share_arrival(k).wait_recv()
    filt_copy = pltpu.make_async_copy(FO, filt_out, out_sem.at[2])
    filt_copy.start()
    tail.wait_send()
    head.wait_send()
    for s in range(m):
        for kind in range(4):
            for d in range(2):
                scatter_copy(s, kind, d).wait_send()
    for k in range(1, N_CTX):
        piece_copy(k).wait_send()
        share_copy(k).wait_send()
    mixed_copy.wait()
    grad_copy.wait()
    filt_copy.wait()


def on_device(inputs, query_weight, key_weight, value_weight, filter_taps, out_grad):
    forward, inverse = transforms()
    vm, dma = pltpu.VMEM, pltpu.SemaphoreType.DMA
    n, m = len(GATHER), len(SCATTER)
    piece = TAPS // N_CTX
    mixed, grad, filt = pl.pallas_call(
        kernel,
        out_shape=(
            jax.ShapeDtypeStruct((BLOCK, GROUP), BF),
            jax.ShapeDtypeStruct((ROWS, D), BF),
            jax.ShapeDtypeStruct((N_CTX, piece, GROUP), F32),
        ),
        in_specs=[pl.BlockSpec(memory_space=pl.ANY)] * 8,
        out_specs=(pl.BlockSpec(memory_space=pl.ANY),) * 3,
        scratch_shapes=[
            vm((SIDE, SIDE, ROWS, D), BF),
            vm((3, D, GROUP), BF),
            vm((3, BLOCK, GROUP), F32),
            vm((BLOCK, GROUP), BF),
            vm((TAPS, GROUP), F32),
            vm((POINTS, POINTS), BF),
            vm((2 * BLOCK + TAPS, POINTS), BF),
            vm((3, BLOCK, GROUP), BF),
            vm((BLOCK, GROUP), BF),
            vm((BLOCK, GROUP), BF),
            vm((TAPS, GROUP), BF),
            vm((TAPS, GROUP), BF),
            vm((POINTS, GROUP), F32),
            vm((POINTS, GROUP), F32),
            vm((POINTS, GROUP), F32),
            vm((POINTS, GROUP), F32),
            vm((BLOCK, GROUP), F32),
            vm((3, BLOCK, GROUP), BF),
            vm((BLOCK, GROUP), BF),
            vm((SIDE, SIDE, ROWS, D), BF),
            vm((SIDE, ROWS, D), BF),
            vm((2, SIDE, ROWS, D), BF),
            vm((ROWS, D), BF),
            vm((2, ROWS, D), BF),
            vm((ROWS, D), BF),
            vm((N_CTX, piece, GROUP), F32),
            vm((N_CTX, piece, GROUP), F32),
            vm((N_CTX, piece, GROUP), F32),
            dma,
            dma((n, 3)),
            dma((4,)),
            dma((3,)),
            dma((n, 4, 2)),
            dma((n, 4, 2)),
            dma((2,)),
            dma((2,)),
            dma((m, 4, 2)),
            dma((m, 4, 2)),
            dma((2, N_CTX)),
            dma((2, N_CTX)),
        ],
        compiler_params=pltpu.CompilerParams(
            collective_id=0, has_side_effects=True, vmem_limit_bytes=60 << 20
        ),
    )(inputs, query_weight, key_weight, value_weight, filter_taps, out_grad, forward, inverse)
    return mixed, grad, filt.reshape(TAPS, GROUP)


def solution(mesh):
    in_specs = (
        P(("ctx", "tp"), None),
        P(None, "tp"),
        P(None, "tp"),
        P(None, "tp"),
        P(None, "tp"),
        P("ctx", "tp"),
    )
    out_specs = (P("ctx", "tp"), P(("ctx", "tp"), None), P(None, "tp"))
    return jax.shard_map(
        on_device, mesh=mesh, in_specs=in_specs, out_specs=out_specs, check_vma=False
    )
```

time: 269 us -> 92.4 us (0.34)
  waiting for transfers between devices: 148 us -> 0 us
  Pallas kernels: 0 us -> 86.6 us
  matrix products: 55.4 us -> 0 us
  other arithmetic: 22.6 us -> 0 us
  local copies, waits for them, and re-layouts: 20.4 us -> 5.01 us
  between operations: 15.1 us -> 0.64 us
  starting transfers between devices: 5.78 us -> 0 us
    pallas_call x0 -> x1, Pallas kernels: none -> 86.6 us  [on_device(): pl.pallas_call(kernel, out_shape=(jax.ShapeDtypeStruct((BLOCK, GROUP), BF...]
    reduce_scatter x1 -> x0, waiting for transfers between devices: 79.5 us -> none  [on_device(): lax.psum_scatter((total + contract(values_rows, value_weight)).astype(jnp...]
    dot_general x6 -> x0, matrix products: 55.4 us -> none  [the longest x3 25 us: contract(): lax.dot_general(left, right, (((1,), (1,)), ((), ())), preferred_element_...]
    all_gather x1 -> x0, waiting for transfers between devices: 49 us -> none  [on_device(): piece = lax.all_gather(inputs, 'tp', axis=0, tiled=True)]
    psum x1 -> x0, waiting for transfers between devices: 18 us -> none  [on_device(): lax.psum(local_taps.astype(jnp.bfloat16), 'ctx').astype(jnp.float32)]
    add x1 -> x0, other arithmetic: 12.3 us -> none  [backward_filter(): total = total + filter_taps[offset] * padded[offset:offset + length]]
    another operation x129 -> x0, local copies, waits for them, and re-layouts: 10.8 us -> none  [tap_products(): return jnp.stack(rows_out)]
    slice x9 -> x0, local copies, waits for them, and re-layouts: 9.49 us -> none  [the longest x7 9.45 us: forward_filter(): total = total + filter_taps[offset] * padded[start:start + length]]
  transfers between devices with their start and end apart: 5 -> 0, of which waited for: 4 -> 0; matrix products, arithmetic and copies ran while one was open for 18% -> 0% of each run, Pallas kernels for 0% -> 0%
where the time goes in v1:
time: 92.4 us; the launch traced here: 92.2 us
  Pallas kernels  86.6 us (94%)
  local copies, waits for them, and re-layouts  5.01 us (5%)
    pallas_call x1, Pallas kernels, on_device(): pl.pallas_call(kernel, out_shape=(jax.ShapeDtypeStruct((BLOCK, GROUP), BF...  86.6 us
    unnamed x3, local copies, waits for them, and re-layouts  5.01 us

profile of v1, /device:TPU:1, one launch (start us, length us, event | category | flops | bytes accessed | tf_op | source)
XLA Modules:
  0.0 92.2 jit_solution(11944710895100220967)
XLA Ops:
  0.6 86.6 %shard_map.103 = (bf16[256,512]{1,0:T(8,128)(2,1)}, bf16[16,8192]{1,0:T(8,128)(2,1)}, f32[8,16,512]{2,1,0:T(8,128)}) custom-call(bf16[16,8192]{1,0:T(8,128)(2,1)} %inp.1, bf16[8192,512]{1,0:T(8,128)(2,1)} %wq.1, bf16[8192,512]{1,0:T(8,128)(2,1)} %wk.1, bf16[8192,512]{1,0:T(8,128)(2,1)} %wv.1, f32[128,512]{1,0:T(8,128)} %taps_in.1, bf16[256,512]{1,0:T(8,128)(2,1)} %og_in.1, ...), custom_call_target="tpu_custom_call" | custom-call | tf_op jit(solution)/shard_map/pallas_call | solution.py:370
  87.2 1.7 %copy.14 = bf16[256,512]{1,0:T(8,128)(2,1)} copy(bf16[256,512]{1,0:T(8,128)(2,1)} %get-tuple-element.12) | data formatting | bytes 524288
  88.9 1.7 %copy.15 = bf16[16,8192]{1,0:T(8,128)(2,1)} copy(bf16[16,8192]{1,0:T(8,128)(2,1)} %get-tuple-element.13) | data formatting | bytes 524288
  90.6 1.7 %copy.16 = f32[128,512]{1,0:T(8,128)} copy(f32[128,512]{1,0:T(8,128)} %bitcast.1) | data formatting | bytes 524288

commit v2 on v1

--- a/solution.py
+++ b/solution.py
@@ -17,8 +17,8 @@
 N_CTX = 8
 FREQ = 192
 POINTS = 2 * FREQ
-GATHER = (2048, 2048, 1536, 1536, 512, 512)
-SCATTER = (512, 512, 1024, 1024, 1024, 1024, 1024, 1024, 512, 512)
+GATHER = (2048, 2048, 2048, 2048)
+SCATTER = (1024, 1024, 2048, 2048, 1024, 1024)
 
 
 def starts(widths):
@@ -44,7 +44,7 @@
     X, W, acc, og, taps, fm, im, qkv, prod, cig, hx, hc, xs, hs, co, cs, conv, G,
     mixed, PB, R1H, R1, R2H, R2, gout, fpart, FR, FO,
     own_sem, w_sem, in_sem, out_sem, ag_send, ag_recv, halo_send, halo_recv, rs_send, rs_recv,
-    f_send, f_recv,
+    f_send, f_recv, met,
 ):
     ctx = lax.axis_index("ctx")
     tp = lax.axis_index("tp")
@@ -73,19 +73,24 @@
         for i, (src, dst) in enumerate(((fwd_in, fm), (taps_in, taps), (inv_in, im), (og_in, og)))
     ]
     own_copies[0].start()
-    for group in loads:
-        for c in group:
-            c.start()
-    for c in small:
-        c.start()
 
     barrier = pltpu.get_barrier_semaphore()
     for dim in range(2):
         for d in range(2):
             pl.semaphore_signal(barrier, inc=1, device_id=near(dim, d), device_id_type=MESH)
-    for k in range(1, N_CTX):
-        pl.semaphore_signal(barrier, inc=1, device_id={"ctx": (ctx + k) % N_CTX}, device_id_type=MESH)
-    pl.semaphore_wait(barrier, 4 + N_CTX - 1)
+    along = ({"ctx": (ctx + 1) % N_CTX}, {"ctx": (ctx + N_CTX - 1) % N_CTX})
+    for to in along:
+        pl.semaphore_signal(barrier, inc=1, device_id=to, device_id_type=MESH)
+    pl.semaphore_wait(barrier, 6)
+
+    def greet(r):
+        for d, to in enumerate(along):
+            pl.semaphore_signal(met.at[r, d], inc=1, device_id=to, device_id_type=MESH)
+
+    def greeted(r):
+        for d in range(2):
+            pl.semaphore_wait(met.at[r, d], 1)
+
     own_copies[0].wait()
 
     def gather_copy(s, kind, d):
@@ -137,6 +142,12 @@
     n = len(GATHER)
     for s in range(n):
         gather_stage(s, 0)
+    greet(0)
+    for c in small:
+        c.start()
+    for group in loads:
+        for c in group:
+            c.start(priority=1)
     for c in small:
         c.wait()
     tap = taps[...]
@@ -151,13 +162,19 @@
     for s in (n - 2, n - 1):
         gather_wait(s, 1)
         gather_stage(s, 2)
+    greeted(0)
+    greet(1)
     gather_stage(0, 3)
     gather_stage(1, 3)
+    greeted(1)
+    greet(2)
     for s in range(n):
         if s + 2 < n:
             gather_stage(s + 2, 3)
         gather_wait(s, 3)
         project(s)
+
+    greeted(2)
 
     qkv[1] = acc[1].astype(BF)
     qkv[2] = acc[2].astype(BF)
@@ -360,6 +377,19 @@
     mixed_copy.wait()
     grad_copy.wait()
     filt_copy.wait()
+
+
+def hand_on(*refs):
+    held, load_sem, store_sem = refs[6:9], refs[9], refs[10]
+    loads = [pltpu.make_async_copy(refs[i], held[i], load_sem.at[i]) for i in range(3)]
+    stores = [pltpu.make_async_copy(held[i], refs[3 + i], store_sem.at[i]) for i in range(3)]
+    for c in loads:
+        c.start()
+    for i in range(3):
+        loads[i].wait()
+        stores[i].start()
+    for c in stores:
+        c.wait()
 
 
 def on_device(inputs, query_weight, key_weight, value_weight, filter_taps, out_grad):
@@ -417,12 +447,20 @@
             dma((m, 4, 2)),
             dma((2, N_CTX)),
             dma((2, N_CTX)),
+            pltpu.SemaphoreType.REGULAR((3, 2)),
         ],
         compiler_params=pltpu.CompilerParams(
             collective_id=0, has_side_effects=True, vmem_limit_bytes=60 << 20
         ),
     )(inputs, query_weight, key_weight, value_weight, filter_taps, out_grad, forward, inverse)
-    return mixed, grad, filt.reshape(TAPS, GROUP)
+    outs = (mixed, grad, filt.reshape(TAPS, GROUP))
+    return pl.pallas_call(
+        hand_on,
+        out_shape=tuple(jax.ShapeDtypeStruct(v.shape, v.dtype) for v in outs),
+        in_specs=[pl.BlockSpec(memory_space=pl.ANY)] * 3,
+        out_specs=(pl.BlockSpec(memory_space=pl.ANY),) * 3,
+        scratch_shapes=[*(vm(v.shape, v.dtype) for v in outs), dma((3,)), dma((3,))],
+    )(*outs)
 
 
 def solution(mesh):

time: 92.4 us -> 79.9 us (0.86)
  the two profiles are of different devices: /device:TPU:1 before, /device:TPU:72 now
where the time goes in v2:
time: 79.9 us; the launch traced here: 79.8 us
  Pallas kernels  79.2 us (99%)
    pallas_call x1, Pallas kernels, on_device(): pl.pallas_call(kernel, out_shape=(jax.ShapeDtypeStruct((BLOCK, GROUP), BF...  77.3 us
    pallas_call x1, Pallas kernels, on_device(): pl.pallas_call(hand_on, out_shape=tuple((jax.ShapeDtypeStruct(v.shape, v....  1.88 us

profile of v2, /device:TPU:72, one launch (start us, length us, event | category | flops | bytes accessed | tf_op | source)
XLA Modules:
  0.0 79.8 jit_solution(1757955208763077297)
XLA Ops:
  0.6 77.3 %shard_map.103 = (bf16[256,512]{1,0:T(8,128)(2,1)}, bf16[16,8192]{1,0:T(8,128)(2,1)}, f32[8,16,512]{2,1,0:T(8,128)}) custom-call(bf16[16,8192]{1,0:T(8,128)(2,1)} %inp.1, bf16[8192,512]{1,0:T(8,128)(2,1)} %wq.1, bf16[8192,512]{1,0:T(8,128)(2,1)} %wk.1, bf16[8192,512]{1,0:T(8,128)(2,1)} %wv.1, f32[128,512]{1,0:T(8,128)} %taps_in.1, bf16[256,512]{1,0:T(8,128)(2,1)} %og_in.1, ...), custom_call_target="tpu_custom_call" | custom-call | tf_op jit(solution)/shard_map/pallas_call | solution.py:400
  77.9 1.9 %shard_map.104 = (bf16[256,512]{1,0:T(8,128)(2,1)}, bf16[16,8192]{1,0:T(8,128)(2,1)}, f32[128,512]{1,0:T(8,128)}) custom-call(bf16[256,512]{1,0:T(8,128)(2,1)} %get-tuple-element.6.refs_0_, bf16[16,8192]{1,0:T(8,128)(2,1)} %get-tuple-element.7.refs_1_, f32[128,512]{1,0:T(8,128)} %bitcast.1), custom_call_target="tpu_custom_call" | custom-call | tf_op jit(solution)/shard_map/pallas_call | solution.py:457

commit v3 on v2

--- a/solution.py
+++ b/solution.py
@@ -42,7 +42,7 @@
     inp, wq, wk, wv, taps_in, og_in, fwd_in, inv_in,
     mixed_out, grad_out, filt_out,
     X, W, acc, og, taps, fm, im, qkv, prod, cig, hx, hc, xs, hs, co, cs, conv, G,
-    mixed, PB, R1H, R1, R2H, R2, gout, fpart, FR, FO,
+    mixed, PB, R1H, R1, R2H, R2, gout, fpart, FR, FO, fout,
     own_sem, w_sem, in_sem, out_sem, ag_send, ag_recv, halo_send, halo_recv, rs_send, rs_recv,
     f_send, f_recv, met,
 ):
@@ -73,6 +73,8 @@
         for i, (src, dst) in enumerate(((fwd_in, fm), (taps_in, taps), (inv_in, im), (og_in, og)))
     ]
     own_copies[0].start()
+    for c in small:
+        c.start(priority=1)
 
     barrier = pltpu.get_barrier_semaphore()
     for dim in range(2):
@@ -123,13 +125,10 @@
         for d in range(2):
             gather_copy(s, kind, d).wait_recv()
 
-    def project(s):
+    def project(s, first, last):
         c0, kw = starts(GATHER)[s], GATHER[s]
-        for c in loads[s]:
-            c.wait()
-
-        def one(i, carry):
-            w = (i + 1) % 3
+
+        def one(w, carry):
             part = dot(X[:, :, :, c0 : c0 + kw].reshape(BLOCK, kw), W[w, c0 : c0 + kw, :])
             if s == 0:
                 acc[w] = part
@@ -137,23 +136,15 @@
                 acc[w] += part
             return carry
 
-        lax.fori_loop(0, 3, one, 0)
+        lax.fori_loop(first, last, one, 0)
 
     n = len(GATHER)
     for s in range(n):
         gather_stage(s, 0)
     greet(0)
-    for c in small:
-        c.start()
     for group in loads:
         for c in group:
             c.start(priority=1)
-    for c in small:
-        c.wait()
-    tap = taps[...]
-    tap_hi = tap.astype(BF)
-    tap_lo = (tap - tap_hi.astype(F32)).astype(BF)
-    hs[...] = dot(fm[:, :TAPS], tap_hi) + dot(fm[:, :TAPS], tap_lo)
     for s in range(n):
         gather_stage(s, 1)
         if s >= 2:
@@ -164,6 +155,12 @@
         gather_stage(s, 2)
     greeted(0)
     greet(1)
+    for c in small:
+        c.wait()
+    tap = taps[...]
+    tap_hi = tap.astype(BF)
+    tap_lo = (tap - tap_hi.astype(F32)).astype(BF)
+    hs[...] = dot(fm[:, :TAPS], tap_hi) + dot(fm[:, :TAPS], tap_lo)
     gather_stage(0, 3)
     gather_stage(1, 3)
     greeted(1)
@@ -172,7 +169,9 @@
         if s + 2 < n:
             gather_stage(s + 2, 3)
         gather_wait(s, 3)
-        project(s)
+        for c in loads[s]:
+            c.wait()
+        project(s, 0 if s < n - 2 else 1, 3)
 
     greeted(2)
 
@@ -184,6 +183,8 @@
         device_id={"ctx": (ctx + 1) % N_CTX}, device_id_type=MESH,
     )
     tail.start()
+    for s in (n - 2, n - 1):
+        project(s, 0, 1)
     qkv[0] = acc[0].astype(BF)
     cig[...] = (og[...].astype(F32) * qkv[0].astype(F32)).astype(BF)
     head = pltpu.make_async_remote_copy(
@@ -329,16 +330,16 @@
         spec = jnp.concatenate(
             [x_re[...] * o_re[...] + x_im[...] * o_im[...], x_im[...] * o_re[...] - x_re[...] * o_im[...]], axis=0
         ).astype(BF)
-        fpart[...] = dot(im[2 * BLOCK :, :], spec).reshape(N_CTX, TAPS // N_CTX, GROUP)
+        fpart[...] = dot(im[2 * BLOCK :, :], spec).astype(BF).reshape(N_CTX, TAPS // N_CTX, GROUP)
         for k in range(1, N_CTX):
             piece_copy(k).start()
 
     def filter_sum():
-        total = fpart[ctx]
+        total = fpart[ctx].astype(F32)
         for k in range(1, N_CTX):
             piece_copy(k).wait_recv()
-            total = total + FR[k]
-        FO[ctx] = total
+            total = total + FR[k].astype(F32)
+        FO[ctx] = total.astype(BF)
         for k in range(1, N_CTX):
             share_copy(k).start()
 
@@ -363,7 +364,8 @@
     grad_copy.start()
     for k in range(1, N_CTX):
         share_arrival(k).wait_recv()
-    filt_copy = pltpu.make_async_copy(FO, filt_out, out_sem.at[2])
+    fout[...] = FO[...].astype(F32)
+    filt_copy = pltpu.make_async_copy(fout, filt_out, out_sem.at[2])
     filt_copy.start()
     tail.wait_send()
     head.wait_send()
@@ -432,8 +434,9 @@
             vm((ROWS, D), BF),
             vm((2, ROWS, D), BF),
             vm((ROWS, D), BF),
-            vm((N_CTX, piece, GROUP), F32),
-            vm((N_CTX, piece, GROUP), F32),
+            vm((N_CTX, piece, GROUP), BF),
+            vm((N_CTX, piece, GROUP), BF),
+            vm((N_CTX, piece, GROUP), BF),
             vm((N_CTX, piece, GROUP), F32),
             dma,
             dma((n, 3)),

time: 79.9 us -> 78.7 us (0.985)
  the two profiles are of different devices: /device:TPU:72 before, /device:TPU:1 now
where the time goes in v3:
time: 78.7 us; the launch traced here: 78.4 us
  Pallas kernels  77.8 us (99%)
    pallas_call x1, Pallas kernels, on_device(): pl.pallas_call(kernel, out_shape=(jax.ShapeDtypeStruct((BLOCK, GROUP), BF...  75.9 us
    pallas_call x1, Pallas kernels, on_device(): pl.pallas_call(hand_on, out_shape=tuple((jax.ShapeDtypeStruct(v.shape, v....  1.88 us

profile of v3, /device:TPU:1, one launch (start us, length us, event | category | flops | bytes accessed | tf_op | source)
XLA Modules:
  0.0 78.4 jit_solution(9463519500873079245)
XLA Ops:
  0.6 75.9 %shard_map.103 = (bf16[256,512]{1,0:T(8,128)(2,1)}, bf16[16,8192]{1,0:T(8,128)(2,1)}, f32[8,16,512]{2,1,0:T(8,128)}) custom-call(bf16[16,8192]{1,0:T(8,128)(2,1)} %inp.1, bf16[8192,512]{1,0:T(8,128)(2,1)} %wq.1, bf16[8192,512]{1,0:T(8,128)(2,1)} %wk.1, bf16[8192,512]{1,0:T(8,128)(2,1)} %wv.1, f32[128,512]{1,0:T(8,128)} %taps_in.1, bf16[256,512]{1,0:T(8,128)(2,1)} %og_in.1, ...), custom_call_target="tpu_custom_call" | custom-call | tf_op jit(solution)/shard_map/pallas_call | solution.py:402
  76.6 1.9 %shard_map.104 = (bf16[256,512]{1,0:T(8,128)(2,1)}, bf16[16,8192]{1,0:T(8,128)(2,1)}, f32[128,512]{1,0:T(8,128)}) custom-call(bf16[256,512]{1,0:T(8,128)(2,1)} %get-tuple-element.6.refs_0_, bf16[16,8192]{1,0:T(8,128)(2,1)} %get-tuple-element.7.refs_1_, f32[128,512]{1,0:T(8,128)} %bitcast.1), custom_call_target="tpu_custom_call" | custom-call | tf_op jit(solution)/shard_map/pallas_call | solution.py:460

commit v4 on v3

--- a/solution.py
+++ b/solution.py
@@ -18,7 +18,7 @@
 FREQ = 192
 POINTS = 2 * FREQ
 GATHER = (2048, 2048, 2048, 2048)
-SCATTER = (1024, 1024, 2048, 2048, 1024, 1024)
+SCATTER = (1024, 1024, 1536, 1536, 1536, 1536)
 
 
 def starts(widths):

time: 78.7 us -> 78.9 us (level)
  no operation moved by 1% of the time
where the time goes in v4:
time: 78.9 us; the launch traced here: 78.8 us
  Pallas kernels  78.1 us (99%)
    pallas_call x1, Pallas kernels, on_device(): pl.pallas_call(kernel, out_shape=(jax.ShapeDtypeStruct((BLOCK, GROUP), BF...  76.2 us
    pallas_call x1, Pallas kernels, on_device(): pl.pallas_call(hand_on, out_shape=tuple((jax.ShapeDtypeStruct(v.shape, v....  1.88 us

profile of v4, /device:TPU:1, one launch (start us, length us, event | category | flops | bytes accessed | tf_op | source)
XLA Modules:
  0.0 78.8 jit_solution(17852927087606913156)
XLA Ops:
  0.6 76.2 %shard_map.103 = (bf16[256,512]{1,0:T(8,128)(2,1)}, bf16[16,8192]{1,0:T(8,128)(2,1)}, f32[8,16,512]{2,1,0:T(8,128)}) custom-call(bf16[16,8192]{1,0:T(8,128)(2,1)} %inp.1, bf16[8192,512]{1,0:T(8,128)(2,1)} %wq.1, bf16[8192,512]{1,0:T(8,128)(2,1)} %wk.1, bf16[8192,512]{1,0:T(8,128)(2,1)} %wv.1, f32[128,512]{1,0:T(8,128)} %taps_in.1, bf16[256,512]{1,0:T(8,128)(2,1)} %og_in.1, ...), custom_call_target="tpu_custom_call" | custom-call | tf_op jit(solution)/shard_map/pallas_call | solution.py:402
  76.9 1.9 %shard_map.104 = (bf16[256,512]{1,0:T(8,128)(2,1)}, bf16[16,8192]{1,0:T(8,128)(2,1)}, f32[128,512]{1,0:T(8,128)}) custom-call(bf16[256,512]{1,0:T(8,128)(2,1)} %get-tuple-element.6.refs_0_, bf16[16,8192]{1,0:T(8,128)(2,1)} %get-tuple-element.7.refs_1_, f32[128,512]{1,0:T(8,128)} %bitcast.1), custom_call_target="tpu_custom_call" | custom-call | tf_op jit(solution)/shard_map/pallas_call | solution.py:460
